TPU v7x, 32 devices: a whole 2x2x4 slice. The times are simulated.
32 devices in a mesh: row: 4 (over x, core), col: 8 (over z, y).
Axes of the slice: x: 2, y: 2, z: 4, core: 2. Of those that a mesh axis runs over, the one named last changes fastest.
Arguments:
- corner: bfloat16 [25600, 25600], P('row', 'col'), may hold values from -32 to 32
- edge: bfloat16 [25600, 25600], P('row', 'col'), may hold values from -32 to 32
- sketch: bfloat16 [25600, 448], P('col'), may hold values from -6 to 6
Outputs:
- corner_new: float32 [400, 400], replicated
- edge_new: float32 [400, 400], replicated
All inputs are finite; a program needn't handle non-finite values.
Results may differ from a plain program's by a relative error of at most 0.0015.
Values may be sent and summed in bfloat16 or wider, within the bound.
A program may use at most 256 MiB of HBM per device.

v0:
```python
import jax
import jax.numpy as jnp
from jax import lax
from jax.sharding import PartitionSpec as P

RANK = 400


def from_root(value, axis, source):
    kept = jnp.where(lax.axis_index(axis) == source, value, 0).astype(value.dtype)
    return lax.psum(kept, axis)


def project(sampled, gram):
    lower = jnp.linalg.cholesky(gram)
    basis = lax.linalg.triangular_solve(
        lower, sampled, left_side=False, lower=True, transpose_a=True
    )
    return basis[:, basis.shape[1] - RANK :].astype(jnp.bfloat16)


def gram_of(sampled):
    return jnp.dot(sampled.T, sampled, precision=lax.Precision.HIGHEST)


def exact_left(narrow_rows, image):
    upper_part = image.astype(jnp.bfloat16)
    lower_part = (image - upper_part.astype(jnp.float32)).astype(jnp.bfloat16)
    first = jnp.dot(narrow_rows.T, upper_part, preferred_element_type=jnp.float32)
    second = jnp.dot(narrow_rows.T, lower_part, preferred_element_type=jnp.float32)
    return first + second


def body(corner, edge, sketch):
    partial_sample = jnp.dot(corner, sketch, preferred_element_type=jnp.float32)
    sampled = lax.psum(partial_sample, "col")
    gram = lax.psum(gram_of(sampled), "row")
    rows_proj = project(sampled, gram)
    width = corner.shape[1]
    ratio = lax.axis_size("col") // lax.axis_size("row")
    col_index = lax.axis_index("col")
    offered = lax.dynamic_slice_in_dim(rows_proj, col_index % ratio * width, width, 0)
    cols_proj = from_root(offered, "row", col_index // ratio)
    corner_part = jnp.dot(corner, cols_proj, preferred_element_type=jnp.float32)
    edge_part = jnp.dot(edge, cols_proj, preferred_element_type=jnp.float32)
    corner_image, edge_image = lax.psum((corner_part, edge_part), "col")
    corner_local = exact_left(rows_proj, corner_image)
    edge_local = exact_left(rows_proj, edge_image)
    corner_new, edge_new = lax.psum((corner_local, edge_local), "row")
    return (corner_new, edge_new)


def solution(mesh):
    placed = (P("row", "col"), P("row", "col"), P("col", None))
    return jax.shard_map(body, mesh=mesh, in_specs=placed, out_specs=(P(), P()), check_vma=False)
```

profile of v0, /device:TPU:0, one launch (start us, length us, event | category | flops | bytes accessed | tf_op | source)
XLA Modules:
  0.0 1422.3 jit_solution(11598771712403457499)
XLA Ops:
  7.2 1.8 copy-done
  9.0 28.2 %fusion.52 = f32[6400,448]{0,1:T(8,128)} fusion(bf16[6400,3200]{1,0:T(8,128)(2,1)} %param.3, bf16[3200,448]{0,1:T(8,128)(2,1)S(1)} %copy-done), kind=kOutput, calls=%fused_computation.95 | convolution fusion | flops 18350080000 | bytes 55296000 | tf_op jit(solution)/shard_map/dot_general | solution.py:35
  37.3 356.6 %all-reduce.11.cloned.1.call-done = f32[6400,448]{0,1:T(8,128)} async-done(((f32[6400,448]{0,1:T(8,128)}), f32[6400,448]{0,1:T(8,128)}) %all-reduce.11.cloned.1.call-update) | async-done | bytes 11468816 | tf_op jit(solution)/shard_map/psum | solution.py:36
  393.9 22.2 %fusion.53 = f32[448,448]{0,1:T(8,128)} fusion(f32[6400,448]{0,1:T(8,128)} %all-reduce.11.cloned.1.call-done), kind=kOutput, calls=%fused_computation.96 | convolution fusion | flops 15414067200 | bytes 12271616 | tf_op jit(solution)/shard_map/dot_general | solution.py:23
  416.1 0.5 all-reduce.15.cloned.1.call-start
  416.8 34.4 %all-reduce.13.cloned.1.call-done = f32[448,448]{0,1:T(8,128)} async-done(((f32[448,448]{0,1:T(8,128)}), f32[448,448]{0,1:T(8,128)}) %all-reduce.13.cloned.1.call-update) | async-done | bytes 802832 | tf_op jit(solution)/shard_map/psum | solution.py:37
  451.1 1.5 copy.6
  452.6 1.4 fusion.28
  454.0 11.7 cholesky.105
  465.8 9.8 custom-call.30
  476.3 11.7 cholesky.219
  488.0 9.9 custom-call.31
  498.2 0.3 convolution_subtract_fusion.3
  498.6 11.7 cholesky.240
  510.3 0.7 compare_reduce_fusion.1
  511.1 9.8 custom-call.32
  521.3 5.8 cholesky.260
  527.2 0.7 compare_reduce_fusion
  527.8 0.6 compare_reduce_fusion.2
  531.2 6.0 while.1
  531.3 0.5 fusion.72
  531.8 1.4 bitcast_dynamic-update-slice_fusion.2
  533.3 0.5 fusion.72
  533.8 1.4 bitcast_dynamic-update-slice_fusion.2
  535.3 0.5 fusion.72
  535.8 1.4 bitcast_dynamic-update-slice_fusion.2
  537.3 39.5 %custom-call.33 = f32[4,128,128]{1,2,0:T(8,128)S(1)} custom-call(f32[4,128,128]{2,1,0:T(8,128)S(1)} %pad_maximum_fusion.3), custom_call_target="InvertDiagBlocksLowerTriangular" | custom-call | tf_op jit(solution)/shard_map/triangular_solve | solution.py:16
  576.8 5.1 fusion.51
  582.0 5.3 convolution_subtract_fusion.1
  587.2 3.2 fusion.50
  590.4 6.7 convolution_subtract_fusion
  597.1 3.2 fusion.49
  600.3 7.4 fusion.6
  607.8 1.6 convolution_convert_fusion
  609.3 0.9 pad_maximum_fusion
  610.3 2.2 copy-done.2
  612.5 1.9 dynamic-slice_select_fusion
  614.5 59.5 %all-reduce.15.cloned.1.call-done = bf16[3200,400]{0,1:T(8,128)(2,1)} async-done(((bf16[3200,400]{0,1:T(8,128)(2,1)}), bf16[3200,400]{0,1:T(8,128)(2,1)}) %all-reduce.15.cloned.1.call-update) | async-done | bytes 2560016 | tf_op jit(solution)/shard_map/psum | solution.py:11
  674.0 29.0 %convolution_bitcast_fusion.1 = f32[6400,400]{0,1:T(8,128)} fusion(bf16[3200,400]{0,1:T(8,128)(2,1)} %all-reduce.15.cloned.1.call-done, bf16[6400,3200]{1,0:T(8,128)(2,1)} %param.3), kind=kOutput, calls=%fused_computation.3 | convolution fusion | flops 16384000000 | bytes 53760000 | tf_op jit(solution)/shard_map/dot_general | solution.py:44
  703.0 25.5 %convolution_bitcast_fusion = f32[6400,400]{0,1:T(8,128)} fusion(bf16[3200,400]{0,1:T(8,128)(2,1)S(1)} %copy-done.4, bf16[6400,3200]{1,0:T(8,128)(2,1)} %param.4), kind=kOutput, calls=%fused_computation.2 | convolution fusion | flops 16384000000 | bytes 53760000 | tf_op jit(solution)/shard_map/dot_general | solution.py:45
  728.6 613.7 %all-reduce.17.cloned.1.call-done = (f32[6400,400]{0,1:T(8,128)}, f32[6400,400]{0,1:T(8,128)}) async-done(((f32[6400,400]{0,1:T(8,128)}, f32[6400,400]{0,1:T(8,128)}), (f32[6400,400]{0,1:T(8,128)}, f32[6400,400]{0,1:T(8,128)})) %all-reduce.17.cloned.1.call-update) | async-done | bytes 20480016 | tf_op jit(solution)/shard_map/psum | solution.py:46
  1342.3 12.1 fusion.12
  1354.4 7.1 fusion.22
  1361.5 2.8 fusion.13
  1364.4 3.7 fusion.25
  1368.1 43.2 %all-reduce.19.cloned.1.call-done = (f32[400,400]{1,0:T(8,128)}, f32[400,400]{1,0:T(8,128)}) async-done(((f32[400,400]{1,0:T(8,128)}, f32[400,400]{1,0:T(8,128)}), (f32[400,400]{1,0:T(8,128)}, f32[400,400]{1,0:T(8,128)})) %all-reduce.19.cloned.1.call-update) | async-done | bytes 1280016 | tf_op jit(solution)/shard_map/psum | solution.py:49
  1411.3 2.1 copy.29
  1413.4 2.1 copy.30
  (54 shorter events, 2.3 us)
Async XLA Ops:
  7.2 1.8 copy-start
  7.2 386.7 %all-reduce.11.cloned.1.call-start = ((), (), s32[]{:S(2)}) async-start(), calls=%async_computation | async-start | bytes 22937600 | tf_op jit(solution)/shard_map/psum | solution.py:36
  37.2 413.9 %all-reduce.13.cloned.1.call-start = ((), (), s32[]{:S(2)}) async-start(), calls=%async_computation.1 | async-start | bytes 1835008 | tf_op jit(solution)/shard_map/psum | solution.py:37
  416.1 257.8 %all-reduce.15.cloned.1.call-start = ((), (), s32[]{:S(2)}) async-start(), calls=%async_computation.2 | async-start | bytes 5120000 | tf_op jit(solution)/shard_map/psum | solution.py:11
  610.3 2.2 copy-start.2
  614.5 727.8 %all-reduce.17.cloned.1.call-start = ((), (), s32[]{:S(2)}) async-start(), calls=%async_computation.3 | async-start | bytes 40960000 | tf_op jit(solution)/shard_map/psum | solution.py:46
  674.0 29.0 %copy-start.4 = (bf16[3200,400]{0,1:T(8,128)(2,1)S(1)}, bf16[3200,400]{0,1:T(8,128)(2,1)}, u32[]{:S(2)}) copy-start(bf16[3200,400]{0,1:T(8,128)(2,1)} %all-reduce.15.cloned.1.call-done) | copy-start | bytes 7680004
  728.5 682.8 %all-reduce.19.cloned.1.call-start = ((), (), s32[]{:S(2)}) async-start(), calls=%async_computation.4 | async-start | bytes 3276800 | tf_op jit(solution)/shard_map/psum | solution.py:49
  1342.3 12.1 copy-start.3
  1342.3 19.2 %slice-start = ((s8[5120000]{0:T(1024)(128)(4,1)}), s8[4194304]{0:T(1024)(128)(4,1)S(1)}, s32[]{:S(2)}) async-start(s8[5120000]{0:T(1024)(128)(4,1)} %bitcast.72), calls=%async_computation.5 | async-start | bytes 8388608
  1342.3 19.2 %slice-start.2 = ((s8[10240000]{0:T(1024)(128)(4,1)}), s8[4194304]{0:T(1024)(128)(4,1)S(1)}, s32[]{:S(2)}) async-start(s8[10240000]{0:T(1024)(128)(4,1)} %bitcast.74), calls=%async_computation.7 | async-start | bytes 8388608
  1342.3 19.2 %slice-start.3 = ((s8[10240000]{0:T(1024)(128)(4,1)}), s8[4194304]{0:T(1024)(128)(4,1)S(1)}, s32[]{:S(2)}) async-start(s8[10240000]{0:T(1024)(128)(4,1)} %bitcast.74), calls=%async_computation.8 | async-start | bytes 8388608
  1354.4 7.1 slice-start.1
  1354.4 7.1 slice-start.4
  1364.4 51.1 %copy-start.1 = (bf16[3200,448]{0,1:T(8,128)(2,1)S(1)}, bf16[3200,448]{0,1:T(8,128)(2,1)}, u32[]{:S(2)}) copy-start(bf16[3200,448]{0,1:T(8,128)(2,1)} %param.5) | copy-start | bytes 8601604
Sparse Core Ops, SparseCore 0:
  37.4 356.4 all-reduce.10
  416.3 34.8 all-reduce.12
  614.6 59.3 all-reduce.14
  728.6 613.5 all-reduce.16
  1368.3 43.0 all-reduce.18
where the time goes:
time: 1430 us; the launch traced here: 1420 us
  waiting for transfers between devices  1110 us (78%)
  matrix products  165 us (12%)
  other arithmetic  117 us (8%)
  between operations  17 us (1%)
  local copies, waits for them, and re-layouts  15.8 us (1%)
    psum x1, waiting for transfers between devices, body(): corner_image, edge_image = lax.psum((corner_part, edge_part), 'col')  614 us
    psum x1, waiting for transfers between devices, body(): sampled = lax.psum(partial_sample, 'col')  357 us
    another operation x14, other arithmetic, project(): lower = jnp.linalg.cholesky(gram)  72.7 us
    psum x1, waiting for transfers between devices, from_root(): return lax.psum(kept, axis)  59.5 us
    psum x1, waiting for transfers between devices, body(): corner_new, edge_new = lax.psum((corner_local, edge_local), 'row')  43.2 us
    another operation x8, other arithmetic, project(): lax.linalg.triangular_solve(lower, sampled, left_side=False, lower=True,...  40.7 us
    psum x1, waiting for transfers between devices, body(): gram = lax.psum(gram_of(sampled), 'row')  34.4 us
    another operation x7, matrix products, project(): lax.linalg.triangular_solve(lower, sampled, left_side=False, lower=True,...  32.4 us
  transfers between devices with their start and end apart: 5, of which 5 were waited for; matrix products, arithmetic and copies ran while one was open for 0% of the time, Pallas kernels for 0%

commit v1 on v0

--- a/solution.py
+++ b/solution.py
@@ -33,7 +33,9 @@
 
 def body(corner, edge, sketch):
     partial_sample = jnp.dot(corner, sketch, preferred_element_type=jnp.float32)
-    sampled = lax.psum(partial_sample, "col")
+    sampled = partial_sample
+    for hop in (1, 2, 4):
+        sampled = sampled + lax.ppermute(sampled, "col", [(dev, dev ^ hop) for dev in range(8)])
     gram = lax.psum(gram_of(sampled), "row")
     rows_proj = project(sampled, gram)
     width = corner.shape[1]

time: 1430 us -> 2080 us (1.45)
  waiting for transfers between devices: 1110 us -> 1740 us
    ppermute x0 -> x3, waiting for transfers between devices: none -> 984 us  [body(): lax.ppermute(sampled, 'col', [(dev, dev ^ hop) for dev in range(8)])]
    psum x1 -> x0, waiting for transfers between devices: 357 us -> none  [body(): sampled = lax.psum(partial_sample, 'col')]
  transfers between devices with their start and end apart: 5 -> 7, of which waited for: 5 -> 7; matrix products, arithmetic and copies ran while one was open for 0% -> 0% of each run, Pallas kernels for 0% -> 0%
where the time goes in v1:
time: 2080 us
  waiting for transfers between devices  1740 us (84%)
  matrix products  163 us (8%)
  other arithmetic  132 us (6%)
    ppermute x3, waiting for transfers between devices, body(): lax.ppermute(sampled, 'col', [(dev, dev ^ hop) for dev in range(8)])  984 us
    psum x1, waiting for transfers between devices, body(): corner_image, edge_image = lax.psum((corner_part, edge_part), 'col')  614 us
    another operation x14, other arithmetic, project(): lower = jnp.linalg.cholesky(gram)  72.7 us
    psum x1, waiting for transfers between devices, from_root(): return lax.psum(kept, axis)  59.5 us
    psum x1, waiting for transfers between devices, body(): corner_new, edge_new = lax.psum((corner_local, edge_local), 'row')  43.2 us
  transfers between devices with their start and end apart: 7, of which 7 were waited for; matrix products, arithmetic and copies ran while one was open for 0% of the time, Pallas kernels for 0%

profile of v1, /device:TPU:0, one launch (start us, length us, event | category | flops | bytes accessed | tf_op | source)
XLA Modules:
  0.0 2076.2 jit_solution(6829279420916596857)
XLA Ops:
  7.2 1.8 copy-done
  9.0 28.2 %fusion.51 = f32[6400,448]{0,1:T(8,128)} fusion(bf16[6400,3200]{1,0:T(8,128)(2,1)} %param.3, bf16[3200,448]{0,1:T(8,128)(2,1)S(1)} %copy-done), kind=kOutput, calls=%fused_computation.97 | convolution fusion | flops 18350080000 | bytes 55296000 | tf_op jit(solution)/shard_map/dot_general | solution.py:35
  37.2 3.0 collective-permute-start
  40.2 246.7 %collective-permute-done = f32[6400,448]{0,1:T(8,128)S(1)} collective-permute-done((f32[6400,448]{0,1:T(8,128)}, f32[6400,448]{0,1:T(8,128)S(1)}, u32[]{:S(2)}, u32[]{:S(2)}) %collective-permute-start) | collective-permute-done | bytes 11468832 | tf_op jit(solution)/shard_map/ppermute | solution.py:38
  286.9 5.2 add.77
  292.0 1.8 collective-permute-start.1
  293.9 246.0 %collective-permute-done.1 = f32[6400,448]{0,1:T(8,128)} collective-permute-done((f32[6400,448]{0,1:T(8,128)S(1)}, f32[6400,448]{0,1:T(8,128)}, u32[]{:S(2)}, u32[]{:S(2)}) %collective-permute-start.1) | collective-permute-done | bytes 11468832 | tf_op jit(solution)/shard_map/ppermute | solution.py:38
  539.8 5.2 add.78
  545.0 2.6 collective-permute-start.2
  547.6 491.1 %collective-permute-done.2 = f32[6400,448]{0,1:T(8,128)} collective-permute-done((f32[6400,448]{0,1:T(8,128)S(1)}, f32[6400,448]{0,1:T(8,128)}, u32[]{:S(2)}, u32[]{:S(2)}) %collective-permute-start.2) | collective-permute-done | bytes 11468832 | tf_op jit(solution)/shard_map/ppermute | solution.py:38
  1038.6 5.2 add.79
  1043.8 4.3 copy-done.2
  1048.1 20.1 fusion.52
  1068.9 36.2 %all-reduce.10.cloned.1.call-done = f32[448,448]{0,1:T(8,128)} async-done(((f32[448,448]{0,1:T(8,128)}), f32[448,448]{0,1:T(8,128)}) %all-reduce.10.cloned.1.call-update) | async-done | bytes 802832 | tf_op jit(solution)/shard_map/psum | solution.py:39
  1105.0 1.5 copy.6
  1106.5 1.4 fusion.28
  1107.9 11.7 cholesky.105
  1119.7 9.8 custom-call.30
  1130.2 11.7 cholesky.219
  1142.0 9.9 custom-call.31
  1152.5 11.7 cholesky.240
  1164.9 9.8 custom-call.32
  1175.2 5.8 cholesky.260
  1185.1 6.0 while.1
  1185.7 1.4 bitcast_dynamic-update-slice_fusion.2
  1187.7 1.4 bitcast_dynamic-update-slice_fusion.2
  1189.7 1.4 bitcast_dynamic-update-slice_fusion.2
  1191.2 39.5 %custom-call.33 = f32[4,128,128]{1,2,0:T(8,128)S(1)} custom-call(f32[4,128,128]{2,1,0:T(8,128)S(1)} %pad_maximum_fusion.3), custom_call_target="InvertDiagBlocksLowerTriangular" | custom-call | tf_op jit(solution)/shard_map/triangular_solve | solution.py:16
  1230.7 5.1 fusion.50
  1235.9 3.2 fusion.37
  1239.1 5.2 fusion.49
  1244.3 4.7 fusion.6
  1249.0 5.3 fusion.48
  1254.2 5.9 fusion
  1260.2 3.1 convolution_convert_fusion
  1264.3 2.2 copy-done.3
  1266.5 1.9 dynamic-slice_select_fusion
  1268.5 59.5 %all-reduce.12.cloned.1.call-done = bf16[3200,400]{0,1:T(8,128)(2,1)} async-done(((bf16[3200,400]{0,1:T(8,128)(2,1)}), bf16[3200,400]{0,1:T(8,128)(2,1)}) %all-reduce.12.cloned.1.call-update) | async-done | bytes 2560016 | tf_op jit(solution)/shard_map/psum | solution.py:11
  1327.9 29.1 %convolution_bitcast_fusion.1 = f32[6400,400]{0,1:T(8,128)} fusion(bf16[3200,400]{0,1:T(8,128)(2,1)} %all-reduce.12.cloned.1.call-done, bf16[6400,3200]{1,0:T(8,128)(2,1)} %param.3), kind=kOutput, calls=%fused_computation.3 | convolution fusion | flops 16384000000 | bytes 53760000 | tf_op jit(solution)/shard_map/dot_general | solution.py:46
  1357.0 25.5 %convolution_bitcast_fusion = f32[6400,400]{0,1:T(8,128)} fusion(bf16[3200,400]{0,1:T(8,128)(2,1)S(1)} %copy-done.5, bf16[6400,3200]{1,0:T(8,128)(2,1)} %param.4), kind=kOutput, calls=%fused_computation.2 | convolution fusion | flops 16384000000 | bytes 53760000 | tf_op jit(solution)/shard_map/dot_general | solution.py:47
  1382.6 613.7 %all-reduce.14.cloned.1.call-done = (f32[6400,400]{0,1:T(8,128)}, f32[6400,400]{0,1:T(8,128)}) async-done(((f32[6400,400]{0,1:T(8,128)}, f32[6400,400]{0,1:T(8,128)}), (f32[6400,400]{0,1:T(8,128)}, f32[6400,400]{0,1:T(8,128)})) %all-reduce.14.cloned.1.call-update) | async-done | bytes 20480016 | tf_op jit(solution)/shard_map/psum | solution.py:48
  1996.3 12.1 fusion.10
  2008.4 7.1 fusion.22
  2015.5 2.8 fusion.11
  2018.4 3.7 fusion.25
  2022.1 43.2 %all-reduce.16.cloned.1.call-done = (f32[400,400]{1,0:T(8,128)}, f32[400,400]{1,0:T(8,128)}) async-done(((f32[400,400]{1,0:T(8,128)}, f32[400,400]{1,0:T(8,128)}), (f32[400,400]{1,0:T(8,128)}, f32[400,400]{1,0:T(8,128)})) %all-reduce.16.cloned.1.call-update) | async-done | bytes 1280016 | tf_op jit(solution)/shard_map/psum | solution.py:51
  2065.3 2.1 copy.28
  2067.4 2.1 copy.29
  (62 shorter events, 7.5 us)
Async XLA Ops:
  7.2 1.8 copy-start
  7.2 1097.8 %all-reduce.10.cloned.1.call-start = ((), (), s32[]{:S(2)}) async-start(), calls=%async_computation | async-start | bytes 1835008 | tf_op jit(solution)/shard_map/psum | solution.py:39
  37.2 249.7 %collective-permute-start = (f32[6400,448]{0,1:T(8,128)}, f32[6400,448]{0,1:T(8,128)S(1)}, u32[]{:S(2)}, u32[]{:S(2)}) collective-permute-start(f32[6400,448]{0,1:T(8,128)} %fusion.51), channel_id=1, source_target_pairs={{0,1},{1,0},{2,3},{3,2},{4,5},{5,4},{6,7},{7,6},{8,9},{9,8},{10,11... | collective-permute-start | bytes 34406408 | tf_op jit(solution)/shard_map/ppermute | solution.py:38
  292.0 247.8 %collective-permute-start.1 = (f32[6400,448]{0,1:T(8,128)S(1)}, f32[6400,448]{0,1:T(8,128)}, u32[]{:S(2)}, u32[]{:S(2)}) collective-permute-start(f32[6400,448]{0,1:T(8,128)S(1)} %add.77), channel_id=1, source_target_pairs={{0,2},{1,3},{2,0},{3,1},{4,6},{5,7},{6,4},{7,5},{8,10},{9,11},{10,... | collective-permute-start | bytes 34406408 | tf_op jit(solution)/shard_map/ppermute | solution.py:38
  545.0 493.6 %collective-permute-start.2 = (f32[6400,448]{0,1:T(8,128)S(1)}, f32[6400,448]{0,1:T(8,128)}, u32[]{:S(2)}, u32[]{:S(2)}) collective-permute-start(f32[6400,448]{0,1:T(8,128)S(1)} %add.78), channel_id=1, source_target_pairs={{0,4},{1,5},{2,6},{3,7},{4,0},{5,1},{6,2},{7,3},{8,12},{9,13},{10,... | collective-permute-start | bytes 34406408 | tf_op jit(solution)/shard_map/ppermute | solution.py:38
  1043.8 4.3 copy-start.2
  1068.2 259.7 %all-reduce.12.cloned.1.call-start = ((), (), s32[]{:S(2)}) async-start(), calls=%async_computation.1 | async-start | bytes 5120000 | tf_op jit(solution)/shard_map/psum | solution.py:11
  1264.2 2.2 copy-start.3
  1268.4 727.9 %all-reduce.14.cloned.1.call-start = ((), (), s32[]{:S(2)}) async-start(), calls=%async_computation.2 | async-start | bytes 40960000 | tf_op jit(solution)/shard_map/psum | solution.py:48
  1327.9 29.1 %copy-start.5 = (bf16[3200,400]{0,1:T(8,128)(2,1)S(1)}, bf16[3200,400]{0,1:T(8,128)(2,1)}, u32[]{:S(2)}) copy-start(bf16[3200,400]{0,1:T(8,128)(2,1)} %all-reduce.12.cloned.1.call-done) | copy-start | bytes 7680004
  1382.5 682.8 %all-reduce.16.cloned.1.call-start = ((), (), s32[]{:S(2)}) async-start(), calls=%async_computation.3 | async-start | bytes 3276800 | tf_op jit(solution)/shard_map/psum | solution.py:51
  1996.3 12.1 copy-start.4
  1996.3 19.2 slice-start
  1996.3 19.2 slice-start.2
  1996.3 19.2 slice-start.3
  2008.4 7.1 slice-start.1
  2008.4 7.1 slice-start.4
  2018.4 51.1 %copy-start.1 = (bf16[3200,448]{0,1:T(8,128)(2,1)S(1)}, bf16[3200,448]{0,1:T(8,128)(2,1)}, u32[]{:S(2)}) copy-start(bf16[3200,448]{0,1:T(8,128)(2,1)} %param.5) | copy-start | bytes 8601604
Sparse Core Ops, SparseCore 0:
  1068.4 36.6 all-reduce.9
  1268.5 59.3 all-reduce.11
  1382.6 613.6 all-reduce.13
  2022.2 43.0 all-reduce.15
